TPU v7x, 128 devices: a whole 4x4x4 slice. The times are simulated.
128 devices in a mesh: section: 4 (over y), seq: 32 (over z, x, core).
Axes of the slice: x: 4, y: 4, z: 4, core: 2. Of those that a mesh axis runs over, the one named last changes fastest.
Arguments:
- layer_input: bfloat16 [4, 2, 2048, 8192], P('section', None, 'seq'), may hold values from -60 to 60
- query_act: bfloat16 [4, 2, 2048, 8192], P('section', None, 'seq'), may hold values from -8 to 8
- key_act: bfloat16 [4, 2, 2048, 1024], P('section', None, 'seq'), may hold values from -6 to 6
- value_act: bfloat16 [4, 2, 2048, 1024], P('section', None, 'seq'), may hold values from -6 to 6
- output_grad: bfloat16 [4, 2, 2048, 8192], P('section', None, 'seq'), may hold values from -24 to 24
- value_weight: bfloat16 [4, 8192, 1024], P('section', 'seq'), may hold values from -0.0625 to 0.0625
- norm_gain: float32 [4, 8192], P('section'), may hold values from 0.1 to 1.9
- top_grad: bfloat16 [2, 2048, 8192], P(None, 'seq'), may hold values from -3 to 3
Outputs:
- input_grad: bfloat16 [4, 2, 2048, 8192], P('section', None, 'seq')
- query_grad: bfloat16 [4, 2, 2048, 8192], P('section', None, 'seq')
- key_grad: bfloat16 [4, 2, 2048, 1024], P('section', None, 'seq')
All inputs are finite; a program needn't handle non-finite values.
Results may differ from a plain program's by a relative error of at most 0.015.
Values may be sent and summed in bfloat16 or wider, within the bound.
No kernel may reach another device: no remote copies, remote signals or barrier semaphores. Data moves between devices by JAX's collectives and lax.ppermute only.
A program may use at most 192 MiB of HBM per device.

v0:
```python
import functools

import jax
import jax.numpy as jnp
from jax import lax
from jax.experimental import pallas as pl
from jax.experimental.pallas import tpu as pltpu
from jax.sharding import PartitionSpec as P

D = 8192
KV_HEADS = 8
HEAD_DIM = 128
BATCH = 2
SEQ = 2048
DEVICES = 32
LOCAL = SEQ // DEVICES
UNIT_HEADS = 4
QCOLS = UNIT_HEADS * HEAD_DIM
UNITS = DEVICES // BATCH
PACK = 2 * QCOLS + 2 * HEAD_DIM
TOK = 128
BLOCKS = SEQ // TOK
CHUNK = 256
CHUNKS = SEQ // CHUNK
SCALE = HEAD_DIM ** (-0.5)
LOG2E = 1.4426950408889634
NEG = -1e30

BF = jnp.bfloat16
F32 = jnp.float32
LAST = (((1,), (1,)), ((), ()))


def pack_body(q_ref, g_ref, k_ref, v_ref, out_ref, sem):
    copies = []
    for dest in range(DEVICES):
        seq, unit = dest // UNITS, dest % UNITS
        head = unit // 2
        for src, width, start, at in (
            (q_ref, QCOLS, unit * QCOLS, 0),
            (g_ref, QCOLS, unit * QCOLS, QCOLS),
            (k_ref, HEAD_DIM, head * HEAD_DIM, 2 * QCOLS),
            (v_ref, HEAD_DIM, head * HEAD_DIM, 2 * QCOLS + HEAD_DIM),
        ):
            copies.append(
                pltpu.make_async_copy(
                    src.at[seq, :, pl.ds(start, width)],
                    out_ref.at[dest, :, pl.ds(at, width)],
                    sem.at[len(copies)],
                )
            )
    for copy in copies:
        copy.start()
    for copy in copies:
        copy.wait()


def pack(q, g, k, v):
    return pl.pallas_call(
        pack_body,
        out_shape=jax.ShapeDtypeStruct((DEVICES, LOCAL, PACK), BF),
        in_specs=[pl.BlockSpec(memory_space=pl.ANY)] * 4,
        out_specs=pl.BlockSpec(memory_space=pl.ANY),
        scratch_shapes=[pltpu.SemaphoreType.DMA((4 * DEVICES,))],
        name="pack",
    )(q, g, k, v)


def unpack_body(in_ref, out_ref, sem):
    copies = []
    for source in range(DEVICES):
        seq, unit = source // UNITS, source % UNITS
        copies.append(
            pltpu.make_async_copy(
                in_ref.at[source],
                out_ref.at[seq, :, pl.ds(unit * QCOLS, QCOLS)],
                sem.at[source],
            )
        )
    for copy in copies:
        copy.start()
    for copy in copies:
        copy.wait()


def unpack(parts):
    return pl.pallas_call(
        unpack_body,
        out_shape=jax.ShapeDtypeStruct((BATCH, LOCAL, D), BF),
        in_specs=[pl.BlockSpec(memory_space=pl.ANY)],
        out_specs=pl.BlockSpec(memory_space=pl.ANY),
        scratch_shapes=[pltpu.SemaphoreType.DMA((DEVICES,))],
        name="unpack",
    )(parts)


def stack_heads(ref):
    return jnp.concatenate(
        [ref[:, h * HEAD_DIM : (h + 1) * HEAD_DIM] for h in range(UNIT_HEADS)], axis=0
    )


def fold(chunk, op):
    return op(chunk.reshape(CHUNK // 8, 8, QCOLS), axis=0)


def probs_body(q_ref, g_ref, k_ref, e_ref, l_ref, dv_ref, s_ref, dv_acc):
    block = pl.program_id(0)
    last = block // 2

    @pl.when(block == 0)
    def _():
        dv_acc[...] = jnp.zeros_like(dv_acc)

    q = stack_heads(q_ref)

    def score(c):
        rows = pl.ds(pl.multiple_of(c * CHUNK, CHUNK), CHUNK)
        return lax.dot_general(k_ref[rows, :], q, LAST, preferred_element_type=F32)

    def sweep_score(c, top):
        s = score(c)
        s_ref[c] = s
        return jnp.maximum(top, fold(s, jnp.max))

    top = lax.fori_loop(0, last, sweep_score, jnp.full((8, QCOLS), NEG, F32))
    s = score(last)
    key_pos = last * CHUNK + lax.broadcasted_iota(jnp.int32, (CHUNK, QCOLS), 0)
    query_pos = block * TOK + lax.broadcasted_iota(jnp.int32, (CHUNK, QCOLS), 1) % TOK
    s = jnp.where(key_pos <= query_pos, s, NEG)
    s_ref[last] = s
    top = jnp.max(jnp.maximum(top, fold(s, jnp.max)), axis=0, keepdims=True)
    factor = SCALE * LOG2E

    def sweep_exp(c, total):
        e = jnp.exp2((s_ref[c] - top) * factor)
        e_ref[c] = e.astype(BF)
        return total + fold(e, jnp.sum)

    total = lax.fori_loop(0, last + 1, sweep_exp, jnp.zeros((8, QCOLS), F32))
    total = jnp.sum(total, axis=0, keepdims=True)
    inverse = 1.0 / total
    l_ref[...] = inverse
    column = jnp.transpose(jnp.broadcast_to(inverse, (HEAD_DIM, QCOLS)))
    g = (stack_heads(g_ref).astype(F32) * column).astype(BF)

    def sweep_dv(c, carry):
        rows = pl.ds(pl.multiple_of(c * CHUNK, CHUNK), CHUNK)
        dv_acc[rows, :] += jnp.dot(e_ref[c], g, preferred_element_type=F32)
        return carry

    lax.fori_loop(0, last + 1, sweep_dv, 0)

    @pl.when(block == BLOCKS - 1)
    def _():
        dv_ref[...] = dv_acc[...].astype(BF)


def attend_probs(packed):
    return pl.pallas_call(
        probs_body,
        grid=(BLOCKS,),
        out_shape=(
            jax.ShapeDtypeStruct((BLOCKS, CHUNKS, CHUNK, QCOLS), BF),
            jax.ShapeDtypeStruct((BLOCKS, 1, QCOLS), F32),
            jax.ShapeDtypeStruct((SEQ, HEAD_DIM), BF),
        ),
        in_specs=[
            pl.BlockSpec((TOK, QCOLS), lambda t: (t, 0)),
            pl.BlockSpec((TOK, QCOLS), lambda t: (t, 1)),
            pl.BlockSpec((SEQ, HEAD_DIM), lambda t: (0, 8)),
        ],
        out_specs=(
            pl.BlockSpec((None, CHUNKS, CHUNK, QCOLS), lambda t: (t, 0, 0, 0)),
            pl.BlockSpec((None, 1, QCOLS), lambda t: (t, 0, 0)),
            pl.BlockSpec((SEQ, HEAD_DIM), lambda t: (0, 0)),
        ),
        scratch_shapes=[
            pltpu.VMEM((CHUNKS, CHUNK, QCOLS), F32),
            pltpu.VMEM((SEQ, HEAD_DIM), F32),
        ],
        compiler_params=pltpu.CompilerParams(vmem_limit_bytes=40 << 20),
        name="probs",
    )(packed, packed, packed)


def grads_body(q_ref, g_ref, k_ref, v_ref, e_ref, l_ref, dq_ref, dk_ref, p_ref, kt_ref, dk_acc):
    block = pl.program_id(0)
    last = block // 2

    @pl.when(block == 0)
    def _():
        dk_acc[...] = jnp.zeros_like(dk_acc)
        for c in range(CHUNKS):
            kt_ref[c] = jnp.transpose(k_ref[c * CHUNK : (c + 1) * CHUNK, :])

    q = stack_heads(q_ref)
    inverse = l_ref[...]
    column = jnp.transpose(jnp.broadcast_to(inverse, (HEAD_DIM, QCOLS)))
    g = (stack_heads(g_ref).astype(F32) * column).astype(BF)

    def sweep_dp(c, total):
        rows = pl.ds(pl.multiple_of(c * CHUNK, CHUNK), CHUNK)
        p = lax.dot_general(v_ref[rows, :], g, LAST, preferred_element_type=F32)
        p_ref[c] = p
        return total + fold(p * e_ref[c].astype(F32), jnp.sum)

    total = lax.fori_loop(0, last + 1, sweep_dp, jnp.zeros((8, QCOLS), F32))
    center = jnp.sum(total, axis=0, keepdims=True) * inverse

    def sweep_ds(c, dq):
        rows = pl.ds(pl.multiple_of(c * CHUNK, CHUNK), CHUNK)
        ds = (e_ref[c].astype(F32) * (p_ref[c] - center)).astype(BF)
        dk_acc[rows, :] += jnp.dot(ds, q, preferred_element_type=F32)
        return dq + jnp.dot(kt_ref[c], ds, preferred_element_type=F32)

    dq = lax.fori_loop(0, last + 1, sweep_ds, jnp.zeros((HEAD_DIM, QCOLS), F32)) * SCALE
    for h in range(UNIT_HEADS):
        cols = slice(h * HEAD_DIM, (h + 1) * HEAD_DIM)
        dq_ref[:, cols] = jnp.transpose(dq[:, cols]).astype(BF)

    @pl.when(block == BLOCKS - 1)
    def _():
        dk_ref[...] = (dk_acc[...] * SCALE).astype(BF)


def attend_grads(packed, e, inverse):
    return pl.pallas_call(
        grads_body,
        grid=(BLOCKS,),
        out_shape=(
            jax.ShapeDtypeStruct((SEQ, QCOLS), BF),
            jax.ShapeDtypeStruct((SEQ, HEAD_DIM), BF),
        ),
        in_specs=[
            pl.BlockSpec((TOK, QCOLS), lambda t: (t, 0)),
            pl.BlockSpec((TOK, QCOLS), lambda t: (t, 1)),
            pl.BlockSpec((SEQ, HEAD_DIM), lambda t: (0, 8)),
            pl.BlockSpec((SEQ, HEAD_DIM), lambda t: (0, 9)),
            pl.BlockSpec((None, CHUNKS, CHUNK, QCOLS), lambda t: (t, 0, 0, 0)),
            pl.BlockSpec((None, 1, QCOLS), lambda t: (t, 0, 0)),
        ],
        out_specs=(
            pl.BlockSpec((TOK, QCOLS), lambda t: (t, 0)),
            pl.BlockSpec((SEQ, HEAD_DIM), lambda t: (0, 0)),
        ),
        scratch_shapes=[
            pltpu.VMEM((CHUNKS, CHUNK, QCOLS), F32),
            pltpu.VMEM((CHUNKS, HEAD_DIM, CHUNK), BF),
            pltpu.VMEM((SEQ, HEAD_DIM), F32),
        ],
        compiler_params=pltpu.CompilerParams(vmem_limit_bytes=40 << 20),
        name="grads",
    )(packed, packed, packed, packed, e, inverse)


ROWS = BATCH * LOCAL
FEATS = 1024


def term_body(vg_ref, w_ref, x_ref, gain_ref, top_ref, flag_ref, out_ref, u_ref, xs_ref, acc):
    step = pl.program_id(0)

    @pl.when(step == 0)
    def _():
        acc[...] = jnp.zeros_like(acc)

    u = lax.dot_general(vg_ref[...], w_ref[...], LAST, preferred_element_type=F32) * gain_ref[...]
    x = x_ref[...].astype(F32)
    u_ref[step] = u
    acc[0] += jnp.sum(x * x, axis=1, keepdims=True)
    acc[1] += jnp.sum(x * u, axis=1, keepdims=True)
    xs_ref[step] = x_ref[...]

    @pl.when(step == pl.num_programs(0) - 1)
    def _():
        r = lax.rsqrt(acc[0] * (1.0 / D) + 1e-05)
        inner = acc[1] * (1.0 / D) * (r * r * r)
        for i in range(D // FEATS):
            cols = slice(i * FEATS, (i + 1) * FEATS)
            term = r * u_ref[i] - xs_ref[i].astype(F32) * inner
            term = term + top_ref[:, cols].astype(F32) * flag_ref[0]
            out_ref[:, cols] = term.astype(BF)


def norm_term(vg, weight, x, gain, top, flag):
    steps = D // FEATS
    return pl.pallas_call(
        term_body,
        grid=(steps,),
        out_shape=jax.ShapeDtypeStruct((ROWS, D), BF),
        in_specs=[
            pl.BlockSpec((ROWS, KV_HEADS * HEAD_DIM), lambda i: (0, 0)),
            pl.BlockSpec((FEATS, KV_HEADS * HEAD_DIM), lambda i: (i, 0)),
            pl.BlockSpec((ROWS, FEATS), lambda i: (0, i)),
            pl.BlockSpec((1, FEATS), lambda i: (0, i)),
            pl.BlockSpec((ROWS, D), lambda i: (0, 0)),
            pl.BlockSpec(memory_space=pltpu.SMEM),
        ],
        out_specs=pl.BlockSpec((ROWS, D), lambda i: (0, 0)),
        scratch_shapes=[
            pltpu.VMEM((steps, ROWS, FEATS), F32),
            pltpu.VMEM((steps, ROWS, FEATS), BF),
            pltpu.VMEM((2, ROWS, 1), F32),
        ],
        compiler_params=pltpu.CompilerParams(vmem_limit_bytes=40 << 20),
        name="term",
    )(vg, weight, x, gain, top, flag)


def exchange(parts):
    return lax.all_to_all(parts, "seq", 0, 0, tiled=True)


def pair_sum(parts):
    both = parts.reshape(BATCH, KV_HEADS, 2, LOCAL, HEAD_DIM).astype(F32)
    total = (both[:, :, 0] + both[:, :, 1]).astype(BF)
    return jnp.concatenate([total[:, g] for g in range(KV_HEADS)], axis=-1)


def local(
    layer_input, query_act, key_act, value_act, output_grad, value_weight, norm_gain, top_grad
):
    weight = lax.all_gather(value_weight[0], "seq", axis=0, tiled=True)
    packed = exchange(pack(query_act[0], output_grad[0], key_act[0], value_act[0]))
    packed = packed.reshape(SEQ, PACK)
    e, inverse, dv = attend_probs(packed)
    dv_parts = exchange(dv.reshape(DEVICES, LOCAL, HEAD_DIM))
    dq, dk = attend_grads(packed, e, inverse)
    value_grad = pair_sum(dv_parts).reshape(ROWS, KV_HEADS * HEAD_DIM)
    sections = lax.axis_size("section")
    here = lax.axis_index("section")
    flag = jnp.where(here == sections - 1, 1.0, 0.0).astype(F32).reshape(1)
    term = norm_term(
        value_grad,
        weight,
        layer_input[0].reshape(ROWS, D),
        norm_gain,
        top_grad.reshape(ROWS, D),
        flag,
    )
    terms = lax.all_to_all(term.reshape(sections, ROWS // sections, D), "section", 0, 0, tiled=True)
    run = terms[sections - 1]
    sums = [run]
    for s in range(sections - 2, -1, -1):
        run = (run.astype(F32) + terms[s].astype(F32)).astype(BF)
        sums.append(run)
    sums = jnp.stack(sums[::-1])
    current = lax.all_to_all(sums, "section", 0, 0, tiled=True)
    dq_parts = exchange(dq.reshape(DEVICES, LOCAL, QCOLS))
    dk_parts = exchange(dk.reshape(DEVICES, LOCAL, HEAD_DIM))
    return (
        current.reshape(1, BATCH, LOCAL, D),
        unpack(dq_parts)[None],
        pair_sum(dk_parts)[None],
    )


def solution(mesh):
    return jax.shard_map(
        local,
        mesh=mesh,
        in_specs=(
            P("section", None, "seq", None),
            P("section", None, "seq", None),
            P("section", None, "seq", None),
            P("section", None, "seq", None),
            P("section", None, "seq", None),
            P("section", "seq", None),
            P("section", None),
            P(None, "seq", None),
        ),
        out_specs=(
            P("section", None, "seq", None),
            P("section", None, "seq", None),
            P("section", None, "seq", None),
        ),
        check_vma=False,
    )
```

profile of v0, /device:TPU:10, one launch (start us, length us, event | category | flops | bytes accessed | tf_op | source)
XLA Modules:
  0.0 505.2 jit_solution(6641970796187944515)
XLA Ops:
  7.2 0.7 all-gather.3.cloned.1.call-update
  7.9 161.1 %pack.1 = bf16[32,64,1280]{2,1,0:T(8,128)(2,1)} custom-call(bf16[2,64,8192]{2,1,0:T(8,128)(2,1)} %bitcast.89, bf16[2,64,8192]{2,1,0:T(8,128)(2,1)} %bitcast.90, bf16[2,64,1024]{2,1,0:T(8,128)(2,1)} %bitcast.94, bf16[2,64,1024]{2,1,0:T(8,128)(2,1)} %bitcast.95), custom_call_target="tpu_custom_call" | custom-call | tf_op jit(solution)/shard_map/pack/pallas_call | solution.py:59
  169.0 69.5 %all_to_all.30 = bf16[32,64,1280]{2,1,0:T(8,128)(2,1)S(1)} all-to-all(bf16[32,64,1280]{2,1,0:T(8,128)(2,1)} %pack.1), channel_id=1, replica_groups=mesh['section'=4,'seq'=32] {'seq'}, dimensions={0} | all-to-all | bytes 10485760 | tf_op jit(solution)/shard_map/all_to_all | solution.py:312
  238.5 44.4 %probs.1 = (bf16[16,8,256,512]{3,2,1,0:T(8,128)(2,1)}, f32[16,1,512]{2,1,0:T(1,128)S(1)}, bf16[2048,128]{1,0:T(8,128)(2,1)}) custom-call(bf16[2048,1280]{1,0:T(8,128)(2,1)S(1)} %bitcast.78, bf16[2048,1280]{1,0:T(8,128)(2,1)S(1)} %bitcast.79, bf16[2048,1280]{1,0:T(8,128)(2,1)S(1)} %bitcast.80), custom_call_target="tpu_custom_call" | custom-call | tf_op jit(solution)/shard_map/probs/pallas_call | solution.py:160
  282.9 5.6 %all-to-all-start.1 = ((bf16[32,64,128]{2,1,0:T(8,128)(2,1)}), bf16[32,64,128]{2,1,0:T(8,128)(2,1)S(1)}, u32[]{:S(2)}, u32[]{:S(2)}) async-start(bf16[32,64,128]{2,1,0:T(8,128)(2,1)} %bitcast.5), calls=%async_computation.1 | async-start | bytes 1048576 | tf_op jit(solution)/shard_map/all_to_all | solution.py:312
  288.5 2.5 copy-done.1
  291.0 45.3 %grads.1 = (bf16[2048,512]{1,0:T(8,128)(2,1)}, bf16[2048,128]{1,0:T(8,128)(2,1)}) custom-call(bf16[2048,1280]{1,0:T(8,128)(2,1)S(1)} %bitcast.81, bf16[2048,1280]{1,0:T(8,128)(2,1)S(1)} %bitcast.82, bf16[2048,1280]{1,0:T(8,128)(2,1)S(1)} %bitcast.83, bf16[2048,1280]{1,0:T(8,128)(2,1)S(1)} %bitcast.84, bf16[16,8,256,512]{3,2,1,0:T(8,128)(2,1)} %get-tuple-element.9.e_ref, ...), custom_call_target="tpu_custom_call" | custom-call | tf_op jit(solution)/shard_map/grads/pallas_call | solution.py:228
  336.3 7.4 %all-to-all-start.5 = ((bf16[32,64,128]{2,1,0:T(8,128)(2,1)}), bf16[32,64,128]{2,1,0:T(8,128)(2,1)S(1)}, u32[]{:S(2)}, u32[]{:S(2)}) async-start(bf16[32,64,128]{2,1,0:T(8,128)(2,1)} %bitcast.25), calls=%async_computation.5 | async-start | bytes 1048576 | tf_op jit(solution)/shard_map/all_to_all | solution.py:312
  343.7 0.1 convert.2
  343.9 0.1 fusion.2
  344.1 1.2 copy-done.2
  345.3 1.6 copy-done.3
  346.9 14.5 %term.1 = bf16[128,8192]{1,0:T(8,128)(2,1)} custom-call(bf16[128,1024]{1,0:T(8,128)(2,1)S(1)} %constant_dynamic-update-slice_fusion.vg_ref, bf16[8192,1024]{1,0:T(8,128)(2,1)} %bitcast.87, bf16[128,8192]{1,0:T(8,128)(2,1)S(1)} %bitcast.85, f32[1,8192]{1,0:T(1,128)S(1)} %copy-done.4, bf16[128,8192]{1,0:T(8,128)(2,1)S(1)} %bitcast.86, f32[1]{0:T(128)} %bitcast.20.flag_ref), custom_call_target="tpu_custom_call" | custom-call | tf_op jit(solution)/shard_map/term/pallas_call | solution.py:288
  361.4 4.9 all-to-all-start.2
  366.3 0.1 convert.3
  366.4 0.1 fusion.3
  366.5 25.0 %all-to-all-done.2 = bf16[4,32,8192]{2,1,0:T(8,128)(2,1)S(1)} async-done(((bf16[4,32,8192]{2,1,0:T(8,128)(2,1)}), bf16[4,32,8192]{2,1,0:T(8,128)(2,1)S(1)}, u32[]{:S(2)}, u32[]{:S(2)}) %all-to-all-start.2) | async-done | bytes 2097184 | tf_op jit(solution)/shard_map/all_to_all | solution.py:342
  391.5 7.4 %all-to-all-start.4 = ((bf16[32,64,512]{2,1,0:T(8,128)(2,1)}), bf16[32,64,512]{2,1,0:T(8,128)(2,1)}, u32[]{:S(2)}, u32[]{:S(2)}) async-start(bf16[32,64,512]{2,1,0:T(8,128)(2,1)} %bitcast.23), calls=%async_computation.4 | async-start | bytes 4194304 | tf_op jit(solution)/shard_map/all_to_all | solution.py:312
  399.0 0.4 add_convert_fusion
  399.4 1.6 pad_maximum_fusion
  400.9 25.9 %all-to-all-done.4.in_ref = bf16[32,64,512]{2,1,0:T(8,128)(2,1)} async-done(((bf16[32,64,512]{2,1,0:T(8,128)(2,1)}), bf16[32,64,512]{2,1,0:T(8,128)(2,1)}, u32[]{:S(2)}, u32[]{:S(2)}) %all-to-all-start.4) | async-done | bytes 2097184 | tf_op jit(solution)/shard_map/all_to_all | solution.py:312
  426.9 5.0 all-to-all-start.3
  432.1 64.9 %unpack.1 = bf16[2,64,8192]{2,1,0:T(8,128)(2,1)} custom-call(bf16[32,64,512]{2,1,0:T(8,128)(2,1)} %all-to-all-done.4.in_ref), custom_call_target="tpu_custom_call" | custom-call | tf_op jit(solution)/shard_map/unpack/pallas_call | solution.py:87
  497.0 1.3 copy.40
  (32 shorter events, 0.4 us)
Async XLA Ops:
  7.2 337.0 %all-gather.3.cloned.1.call-start = ((), (), s32[]{:S(2)}) async-start(), calls=%async_computation.6 | async-start | bytes 17301504 | tf_op jit(solution)/shard_map/all_gather | solution.py:324
  238.5 44.4 %copy-start = (bf16[32,64,1280]{2,1,0:T(8,128)(2,1)}, bf16[32,64,1280]{2,1,0:T(8,128)(2,1)S(1)}, u32[]{:S(2)}) copy-start(bf16[32,64,1280]{2,1,0:T(8,128)(2,1)S(1)} %all_to_all.30) | copy-start | bytes 15728644
  282.9 53.5 %all-to-all-start.1 = ((bf16[32,64,128]{2,1,0:T(8,128)(2,1)}), bf16[32,64,128]{2,1,0:T(8,128)(2,1)S(1)}, u32[]{:S(2)}, u32[]{:S(2)}) async-start(bf16[32,64,128]{2,1,0:T(8,128)(2,1)} %bitcast.5), calls=%async_computation.1 | async-start | bytes 1048576 | tf_op jit(solution)/shard_map/all_to_all | solution.py:312
  288.5 2.5 copy-start.1
  336.3 25.1 %all-to-all-start.5 = ((bf16[32,64,128]{2,1,0:T(8,128)(2,1)}), bf16[32,64,128]{2,1,0:T(8,128)(2,1)S(1)}, u32[]{:S(2)}, u32[]{:S(2)}) async-start(bf16[32,64,128]{2,1,0:T(8,128)(2,1)} %bitcast.25), calls=%async_computation.5 | async-start | bytes 1048576 | tf_op jit(solution)/shard_map/all_to_all | solution.py:312
  343.7 1.6 copy-start.2
  343.7 1.6 copy-start.4
  345.3 1.6 copy-start.3
  361.4 30.1 %all-to-all-start.2 = ((bf16[4,32,8192]{2,1,0:T(8,128)(2,1)}), bf16[4,32,8192]{2,1,0:T(8,128)(2,1)S(1)}, u32[]{:S(2)}, u32[]{:S(2)}) async-start(bf16[4,32,8192]{2,1,0:T(8,128)(2,1)} %bitcast.21), calls=%async_computation.2 | async-start | bytes 4194304 | tf_op jit(solution)/shard_map/all_to_all | solution.py:342
  391.5 35.4 %all-to-all-start.4 = ((bf16[32,64,512]{2,1,0:T(8,128)(2,1)}), bf16[32,64,512]{2,1,0:T(8,128)(2,1)}, u32[]{:S(2)}, u32[]{:S(2)}) async-start(bf16[32,64,512]{2,1,0:T(8,128)(2,1)} %bitcast.23), calls=%async_computation.4 | async-start | bytes 4194304 | tf_op jit(solution)/shard_map/all_to_all | solution.py:312
  426.9 70.1 %all-to-all-start.3 = ((bf16[4,32,8192]{2,1,0:T(8,128)(2,1)}), bf16[4,32,8192]{2,1,0:T(8,128)(2,1)S(1)}, u32[]{:S(2)}, u32[]{:S(2)}) async-start(bf16[4,32,8192]{2,1,0:T(8,128)(2,1)} %pad_maximum_fusion), calls=%async_computation.3 | async-start | bytes 4194304 | tf_op jit(solution)/shard_map/all_to_all | solution.py:349
  432.1 64.9 %copy-start.5 = (bf16[2,64,1024]{2,1,0:T(8,128)(2,1)}, bf16[2,64,1024]{2,1,0:T(8,128)(2,1)S(1)}, u32[]{:S(2)}) copy-start(bf16[2,64,1024]{2,1,0:T(8,128)(2,1)S(1)} %constant_dynamic-update-slice_fusion.8) | copy-start | bytes 786436
Sparse Core Ops, SparseCore 0:
  10.3 74.8 all-gather.2
where the time goes:
time: 508 us; the launch traced here: 505 us
  Pallas kernels  330 us (65%)
  blocking collectives  69.5 us (14%)
  waiting for transfers between devices  51.6 us (10%)
  starting transfers between devices  30.4 us (6%)
  between operations  14.3 us (3%)
  local copies, waits for them, and re-layouts  6.86 us (1%)
    pallas_call x1, Pallas kernels, pack(): pl.pallas_call(pack_body, out_shape=jax.ShapeDtypeStruct((DEVICES, LOCAL,...  161 us
    all_to_all x1, blocking collectives, exchange(): return lax.all_to_all(parts, 'seq', 0, 0, tiled=True)  69.5 us
    pallas_call x1, Pallas kernels, unpack(): pl.pallas_call(unpack_body, out_shape=jax.ShapeDtypeStruct((BATCH, LOCAL,...  64.9 us
    pallas_call x1, Pallas kernels, attend_grads(): pl.pallas_call(grads_body, grid=(BLOCKS,), out_shape=(jax.ShapeDtypeStruc...  45.3 us
    pallas_call x1, Pallas kernels, attend_probs(): pl.pallas_call(probs_body, grid=(BLOCKS,), out_shape=(jax.ShapeDtypeStruc...  44.4 us
    all_to_all x3, waiting for transfers between devices, exchange(): return lax.all_to_all(parts, 'seq', 0, 0, tiled=True)  25.9 us
    all_to_all x1, waiting for transfers between devices, local(): lax.all_to_all(term.reshape(sections, ROWS // sections, D), 'section', 0,...  25 us
    all_to_all x3, starting transfers between devices, exchange(): return lax.all_to_all(parts, 'seq', 0, 0, tiled=True)  20.4 us
  transfers between devices with their start and end apart: 6, of which 2 were waited for; matrix products, arithmetic and copies ran while one was open for 1% of the time, Pallas kernels for 65%

commit v1 on v0

v1 whole, which is shorter than its diff:
```python
import jax
import jax.numpy as jnp
from jax import lax
from jax.experimental import pallas as pl
from jax.experimental.pallas import tpu as pltpu
from jax.sharding import PartitionSpec as P

D = 8192
KV_HEADS = 8
HEAD_DIM = 128
BATCH = 2
SEQ = 2048
DEVICES = 32
LOCAL = SEQ // DEVICES
UNIT_HEADS = 4
QCOLS = UNIT_HEADS * HEAD_DIM
UNITS = DEVICES // BATCH
PACK = QCOLS + HEAD_DIM
STEP_UNITS = 4
TOK = 128
BLOCKS = SEQ // TOK
CHUNK = 256
CHUNKS = SEQ // CHUNK
HALF = BLOCKS // 2
HALF_CHUNKS = CHUNKS // 2
HALF = BLOCKS // 2
HALF_CHUNKS = CHUNKS // 2
SCALE = HEAD_DIM ** (-0.5)
LOG2E = 1.4426950408889634
NEG = -1e30

BF = jnp.bfloat16
F32 = jnp.float32
LAST = (((1,), (1,)), ((), ()))


PARAMS = pltpu.CompilerParams(vmem_limit_bytes=60 << 20)


def cost(us):
    return pl.CostEstimate(flops=int(us * 1e9), transcendentals=0, bytes_accessed=0)


def pack_body(wide_ref, slim_ref, out_ref):
    for unit in range(STEP_UNITS):
        cols = slice(unit * QCOLS, (unit + 1) * QCOLS)
        kv = slice(unit // 2 * HEAD_DIM, (unit // 2 + 1) * HEAD_DIM)
        out_ref[unit, :, :QCOLS] = wide_ref[:, cols]
        out_ref[unit, :, QCOLS:] = slim_ref[:, kv]


def pack(wide, slim):
    per_seq = UNITS // STEP_UNITS
    return pl.pallas_call(
        pack_body,
        grid=(BATCH, per_seq),
        out_shape=jax.ShapeDtypeStruct((DEVICES, LOCAL, PACK), BF),
        in_specs=[
            pl.BlockSpec((None, LOCAL, STEP_UNITS * QCOLS), lambda b, i: (b, 0, i)),
            pl.BlockSpec((None, LOCAL, STEP_UNITS // 2 * HEAD_DIM), lambda b, i: (b, 0, i)),
        ],
        out_specs=pl.BlockSpec((STEP_UNITS, LOCAL, PACK), lambda b, i: (b * per_seq + i, 0, 0)),
        cost_estimate=cost(3),
        compiler_params=PARAMS,
        name="pack",
    )(wide, slim)


def unpack_body(in_ref, wide_ref, slim_ref):
    for unit in range(STEP_UNITS):
        wide_ref[:, unit * QCOLS : (unit + 1) * QCOLS] = in_ref[unit, :, :QCOLS]
    for head in range(STEP_UNITS // 2):
        total = in_ref[2 * head, :, QCOLS:].astype(F32) + in_ref[2 * head + 1, :, QCOLS:].astype(F32)
        slim_ref[:, head * HEAD_DIM : (head + 1) * HEAD_DIM] = total.astype(BF)


def unpack(parts):
    per_seq = UNITS // STEP_UNITS
    return pl.pallas_call(
        unpack_body,
        grid=(BATCH, per_seq),
        out_shape=(
            jax.ShapeDtypeStruct((BATCH, LOCAL, D), BF),
            jax.ShapeDtypeStruct((BATCH, LOCAL, KV_HEADS * HEAD_DIM), BF),
        ),
        in_specs=[pl.BlockSpec((STEP_UNITS, LOCAL, PACK), lambda b, i: (b * per_seq + i, 0, 0))],
        out_specs=(
            pl.BlockSpec((None, LOCAL, STEP_UNITS * QCOLS), lambda b, i: (b, 0, i)),
            pl.BlockSpec((None, LOCAL, STEP_UNITS // 2 * HEAD_DIM), lambda b, i: (b, 0, i)),
        ),
        cost_estimate=cost(5),
        compiler_params=PARAMS,
        name="unpack",
    )(parts)


def stack_heads(ref):
    return jnp.concatenate(
        [ref[:, h * HEAD_DIM : (h + 1) * HEAD_DIM] for h in range(UNIT_HEADS)], axis=0
    )


def fold(chunk, op):
    return op(chunk.reshape(CHUNK // 8, 8, QCOLS), axis=0)


def join(a, b, op):
    return b if a is None else op(a, b)


def chunk_rows(c):
    return slice(c * CHUNK, (c + 1) * CHUNK)


def probs_body(q_ref, k_ref, low_ref, high_ref, l_ref, s_ref):
    block = pl.program_id(0)

    for last in range(CHUNKS):
        e_ref = low_ref if last < HALF_CHUNKS else high_ref

        @pl.when(block // 2 == last)
        def _():
            q = stack_heads(q_ref)
            top = None
            for c in range(last + 1):
                s = lax.dot_general(k_ref[chunk_rows(c), :], q, LAST, preferred_element_type=F32)
                if c == last:
                    key_pos = c * CHUNK + lax.broadcasted_iota(jnp.int32, (CHUNK, QCOLS), 0)
                    query_pos = block * TOK + lax.broadcasted_iota(
                        jnp.int32, (CHUNK, QCOLS), 1
                    ) % TOK
                    s = jnp.where(key_pos <= query_pos, s, NEG)
                s_ref[c] = s
                top = join(top, fold(s, jnp.max), jnp.maximum)
            top = jnp.max(top, axis=0, keepdims=True)
            total = None
            for c in range(last + 1):
                e = jnp.exp2((s_ref[c] - top) * (SCALE * LOG2E))
                e_ref[c] = e.astype(BF)
                total = join(total, fold(e, jnp.sum), jnp.add)
            l_ref[...] = 1.0 / jnp.sum(total, axis=0, keepdims=True)


LOW_SPEC = pl.BlockSpec(
    (None, HALF_CHUNKS, CHUNK, QCOLS), lambda t: (jnp.minimum(t, HALF - 1), 0, 0, 0)
)
HIGH_SPEC = pl.BlockSpec(
    (None, CHUNKS, CHUNK, QCOLS), lambda t: (jnp.maximum(t - HALF, 0), 0, 0, 0)
)
STAT_SPEC = pl.BlockSpec((None, 1, QCOLS), lambda t: (t, 0, 0))


def attend_probs(packed):
    return pl.pallas_call(
        probs_body,
        grid=(BLOCKS,),
        out_shape=(
            jax.ShapeDtypeStruct((HALF, HALF_CHUNKS, CHUNK, QCOLS), BF),
            jax.ShapeDtypeStruct((HALF, CHUNKS, CHUNK, QCOLS), BF),
            jax.ShapeDtypeStruct((BLOCKS, 1, QCOLS), F32),
        ),
        in_specs=[
            pl.BlockSpec((TOK, QCOLS), lambda t: (t, 0)),
            pl.BlockSpec((SEQ, HEAD_DIM), lambda t: (0, UNIT_HEADS)),
        ],
        out_specs=(LOW_SPEC, HIGH_SPEC, STAT_SPEC),
        scratch_shapes=[pltpu.VMEM((CHUNKS, CHUNK, QCOLS), F32)],
        compiler_params=PARAMS,
        cost_estimate=cost(18),
        name="probs",
    )(packed, packed)


def scaled_grad(g_ref, l_ref):
    column = jnp.transpose(jnp.broadcast_to(l_ref[...], (HEAD_DIM, QCOLS)))
    return (stack_heads(g_ref).astype(F32) * column).astype(BF)


def values_body(g_ref, low_ref, high_ref, l_ref, dv_ref, acc):
    block = pl.program_id(0)

    @pl.when(block == 0)
    def _():
        acc[...] = jnp.zeros_like(acc)

    for last in range(CHUNKS):
        e_ref = low_ref if last < HALF_CHUNKS else high_ref

        @pl.when(block // 2 == last)
        def _():
            g = scaled_grad(g_ref, l_ref)
            for c in range(last + 1):
                acc[chunk_rows(c), :] += jnp.dot(e_ref[c], g, preferred_element_type=F32)

    @pl.when(block == BLOCKS - 1)
    def _():
        dv_ref[...] = acc[...].astype(BF)


def attend_values(packed, low, high, inverse):
    return pl.pallas_call(
        values_body,
        grid=(BLOCKS,),
        out_shape=jax.ShapeDtypeStruct((SEQ, HEAD_DIM), BF),
        in_specs=[
            pl.BlockSpec((TOK, QCOLS), lambda t: (t, 0)),
            LOW_SPEC,
            HIGH_SPEC,
            STAT_SPEC,
        ],
        out_specs=pl.BlockSpec((SEQ, HEAD_DIM), lambda t: (0, 0)),
        scratch_shapes=[pltpu.VMEM((SEQ, HEAD_DIM), F32)],
        compiler_params=PARAMS,
        cost_estimate=cost(10),
        name="values",
    )(packed, low, high, inverse)


def grads_body(
    q_ref, g_ref, k_ref, v_ref, low_ref, high_ref, l_ref, out_ref, p_ref, kt_ref, acc
):
    step = pl.program_id(0)
    block = BLOCKS - 1 - step

    @pl.when(step == 0)
    def _():
        acc[...] = jnp.zeros_like(acc)
        for c in range(CHUNKS):
            kt_ref[c] = jnp.transpose(k_ref[chunk_rows(c), :])

    for last in range(CHUNKS):
        e_ref = low_ref if last < HALF_CHUNKS else high_ref

        @pl.when(block // 2 == last)
        def _():
            q = stack_heads(q_ref)
            g = scaled_grad(g_ref, l_ref)
            total = None
            for c in range(last + 1):
                p = lax.dot_general(v_ref[chunk_rows(c), :], g, LAST, preferred_element_type=F32)
                p_ref[c] = p
                total = join(total, fold(p * e_ref[c].astype(F32), jnp.sum), jnp.add)
            center = jnp.sum(total, axis=0, keepdims=True) * l_ref[...]
            dq = None
            for c in range(last + 1):
                ds = (e_ref[c].astype(F32) * (p_ref[c] - center)).astype(BF)
                acc[chunk_rows(c), :] += jnp.dot(ds, q, preferred_element_type=F32)
                dq = join(dq, jnp.dot(kt_ref[c], ds, preferred_element_type=F32), jnp.add)
            dq = dq * SCALE
            for h in range(UNIT_HEADS):
                cols = slice(h * HEAD_DIM, (h + 1) * HEAD_DIM)
                out_ref[:, cols] = jnp.transpose(dq[:, cols]).astype(BF)

    rows = pl.ds(pl.multiple_of(block * TOK, TOK), TOK)
    out_ref[:, QCOLS:] = (acc[rows, :] * SCALE).astype(BF)


def backward(spec):
    index = spec.index_map
    return pl.BlockSpec(spec.block_shape, lambda t: index(BLOCKS - 1 - t))


def attend_grads(query_key, grad_value, low, high, inverse):
    wide = backward(pl.BlockSpec((TOK, QCOLS), lambda t: (t, 0)))
    slim = pl.BlockSpec((SEQ, HEAD_DIM), lambda t: (0, UNIT_HEADS))
    return pl.pallas_call(
        grads_body,
        grid=(BLOCKS,),
        out_shape=jax.ShapeDtypeStruct((SEQ, PACK), BF),
        in_specs=[wide, wide, slim, slim]
        + [backward(LOW_SPEC), backward(HIGH_SPEC), backward(STAT_SPEC)],
        out_specs=backward(pl.BlockSpec((TOK, PACK), lambda t: (t, 0))),
        scratch_shapes=[
            pltpu.VMEM((CHUNKS, CHUNK, QCOLS), F32),
            pltpu.VMEM((CHUNKS, HEAD_DIM, CHUNK), BF),
            pltpu.VMEM((SEQ, HEAD_DIM), F32),
        ],
        compiler_params=PARAMS,
        cost_estimate=cost(27),
        name="grads",
    )(query_key, grad_value, query_key, grad_value, low, high, inverse)


ROWS = BATCH * LOCAL
FEATS = 1024
SECTIONS = 4
PART = ROWS // SECTIONS


def pair_sums(parts_ref, emit):
    for seq in range(BATCH):
        for head in range(KV_HEADS):
            first = seq * UNITS + 2 * head
            total = parts_ref[first].astype(F32) + parts_ref[first + 1].astype(F32)
            emit(seq, slice(head * HEAD_DIM, (head + 1) * HEAD_DIM), total.astype(BF))


def term_body(here_ref, parts_ref, w_ref, x_ref, gain_ref, top_ref, *refs):
    out_refs, (vg_ref, u_ref, xs_ref, acc) = refs[:SECTIONS], refs[SECTIONS:]
    step = pl.program_id(0)

    @pl.when(step == 0)
    def _():
        acc[...] = jnp.zeros_like(acc)

        def emit(seq, cols, value):
            vg_ref[seq * LOCAL : (seq + 1) * LOCAL, cols] = value

        pair_sums(parts_ref, emit)

    u = lax.dot_general(vg_ref[...], w_ref[...], LAST, preferred_element_type=F32) * gain_ref[...]
    x = x_ref[...].astype(F32)
    u_ref[step] = u
    acc[0] += jnp.sum(x * x, axis=1, keepdims=True)
    acc[1] += jnp.sum(x * u, axis=1, keepdims=True)
    xs_ref[step] = x_ref[...]

    @pl.when(step == pl.num_programs(0) - 1)
    def _():
        here = here_ref[0]
        flag = jnp.where(here == SECTIONS - 1, 1.0, 0.0).astype(F32)
        r = lax.rsqrt(acc[0] * (1.0 / D) + 1e-05)
        inner = acc[1] * (1.0 / D) * (r * r * r)
        acc[0] = r
        acc[1] = inner
        for k in range(SECTIONS):
            rows = pl.ds(pl.multiple_of(((here + k) % SECTIONS) * PART, PART), PART)
            r = acc[0, rows, :]
            inner = acc[1, rows, :]
            for i in range(D // FEATS):
                cols = slice(i * FEATS, (i + 1) * FEATS)
                term = r * u_ref[i, rows, :] - xs_ref[i, rows, :].astype(F32) * inner
                term = term + top_ref[rows, cols].astype(F32) * flag
                out_refs[k][:, cols] = term.astype(BF)


def norm_term(here, parts, weight, x, gain, top):
    steps = D // FEATS
    return pl.pallas_call(
        term_body,
        grid=(steps,),
        out_shape=tuple(jax.ShapeDtypeStruct((PART, D), BF) for _ in range(SECTIONS)),
        in_specs=[
            pl.BlockSpec(memory_space=pltpu.SMEM),
            pl.BlockSpec((DEVICES, LOCAL, HEAD_DIM), lambda i: (0, 0, 0)),
            pl.BlockSpec((FEATS, KV_HEADS * HEAD_DIM), lambda i: (i, 0)),
            pl.BlockSpec((ROWS, FEATS), lambda i: (0, i)),
            pl.BlockSpec((1, FEATS), lambda i: (0, i)),
            pl.BlockSpec((ROWS, D), lambda i: (0, 0)),
        ],
        out_specs=tuple(pl.BlockSpec((PART, D), lambda i: (0, 0)) for _ in range(SECTIONS)),
        scratch_shapes=[
            pltpu.VMEM((ROWS, KV_HEADS * HEAD_DIM), BF),
            pltpu.VMEM((steps, ROWS, FEATS), F32),
            pltpu.VMEM((steps, ROWS, FEATS), BF),
            pltpu.VMEM((2, ROWS, 1), F32),
        ],
        compiler_params=PARAMS,
        cost_estimate=cost(12),
        name="term",
    )(here, parts, weight, x, gain, top)


def sums_body(here_ref, *refs):
    parts, outs = refs[:SECTIONS], refs[SECTIONS:]
    here = here_ref[0]
    place = [(here - j) % SECTIONS for j in range(SECTIONS)]
    values = [part[...].astype(F32) for part in parts]
    for k in range(SECTIONS):
        total = values[k]
        for j in range(SECTIONS):
            if j != k:
                total = total + values[j] * jnp.where(place[j] > place[k], 1.0, 0.0).astype(F32)
        outs[k][...] = total.astype(BF)


def suffix_sums(here, parts):
    cols = D // 4
    spec = pl.BlockSpec((PART, cols), lambda i: (0, i))
    return pl.pallas_call(
        sums_body,
        grid=(D // cols,),
        out_shape=tuple(jax.ShapeDtypeStruct((PART, D), BF) for _ in range(SECTIONS)),
        in_specs=[pl.BlockSpec(memory_space=pltpu.SMEM)] + [spec] * SECTIONS,
        out_specs=(spec,) * SECTIONS,
        cost_estimate=cost(2),
        compiler_params=PARAMS,
        name="suffix_sums",
    )(here, *parts)


def place_body(here_ref, *refs):
    parts, out_ref = refs[:SECTIONS], refs[SECTIONS]
    here = here_ref[0]
    for k in range(SECTIONS):
        rows = pl.ds(pl.multiple_of(((here + k) % SECTIONS) * PART, PART), PART)
        out_ref[rows, :] = parts[k][...]


def place(here, parts):
    cols = D // 4
    spec = pl.BlockSpec((PART, cols), lambda i: (0, i))
    return pl.pallas_call(
        place_body,
        grid=(D // cols,),
        out_shape=jax.ShapeDtypeStruct((ROWS, D), BF),
        in_specs=[pl.BlockSpec(memory_space=pltpu.SMEM)] + [spec] * SECTIONS,
        out_specs=pl.BlockSpec((ROWS, cols), lambda i: (0, i)),
        cost_estimate=cost(2),
        compiler_params=PARAMS,
        name="place",
    )(here, *parts)


def exchange(parts):
    return lax.all_to_all(parts, "seq", 0, 0, tiled=True)


def turn(array, by):
    pairs = [(i, (i + by) % SECTIONS) for i in range(SECTIONS)]
    return lax.ppermute(array, "section", pairs)


def local(
    layer_input, query_act, key_act, value_act, output_grad, value_weight, norm_gain, top_grad
):
    weight = lax.all_gather(value_weight[0], "seq", axis=0, tiled=True)
    query_key = exchange(pack(query_act[0], key_act[0])).reshape(SEQ, PACK)
    grad_value = exchange(pack(output_grad[0], value_act[0])).reshape(SEQ, PACK)
    low, high, inverse = attend_probs(query_key)
    dv = attend_values(grad_value, low, high, inverse)
    dv_parts = exchange(dv.reshape(DEVICES, LOCAL, HEAD_DIM))
    grads = attend_grads(query_key, grad_value, low, high, inverse)
    grads_back = exchange(grads.reshape(DEVICES, LOCAL, PACK))
    here = lax.axis_index("section").astype(jnp.int32).reshape(1)
    terms = norm_term(
        here,
        dv_parts,
        weight,
        layer_input[0].reshape(ROWS, D),
        norm_gain,
        top_grad.reshape(ROWS, D),
    )
    arrived = [terms[0]] + [turn(terms[k], k) for k in range(1, SECTIONS)]
    sums = suffix_sums(here, arrived)
    back = [sums[0]] + [turn(sums[k], -k) for k in range(1, SECTIONS)]
    current = place(here, back)
    query_grad, key_grad = unpack(grads_back)
    return current.reshape(1, BATCH, LOCAL, D), query_grad[None], key_grad[None]


def solution(mesh):
    return jax.shard_map(
        local,
        mesh=mesh,
        in_specs=(
            P("section", None, "seq", None),
            P("section", None, "seq", None),
            P("section", None, "seq", None),
            P("section", None, "seq", None),
            P("section", None, "seq", None),
            P("section", "seq", None),
            P("section", None),
            P(None, "seq", None),
        ),
        out_specs=(
            P("section", None, "seq", None),
            P("section", None, "seq", None),
            P("section", None, "seq", None),
        ),
        check_vma=False,
    )
```

time: 508 us -> 281 us (0.55)
  Pallas kernels: 330 us -> 108 us
  blocking collectives: 69.5 us -> 0 us
  waiting for transfers between devices: 51.6 us -> 115 us
  starting transfers between devices: 30.4 us -> 37 us
    pallas_call x4 -> x8, Pallas kernels: 286 us -> 87.2 us  [the longest x1 27.4 us: attend_grads(): pl.pallas_call(grads_body, grid=(BLOCKS,), out_shape=jax.ShapeDtypeStruct...]
    all_to_all x1 -> x0, blocking collectives: 69.5 us -> none  [exchange(): return lax.all_to_all(parts, 'seq', 0, 0, tiled=True)]
    all_to_all x3 -> x4, waiting for transfers between devices: 25.9 us -> 76.4 us  [exchange(): return lax.all_to_all(parts, 'seq', 0, 0, tiled=True)]
    ppermute x0 -> x6, waiting for transfers between devices: none -> 37.5 us  [turn(): return lax.ppermute(array, 'section', pairs)]
    all_to_all x2 -> x0, waiting for transfers between devices: 25 us -> none  [the longest x1 25 us: local(): lax.all_to_all(term.reshape(sections, ROWS // sections, D), 'section', 0,...]
    pallas_call x1, Pallas kernels: 44.4 us -> 20.4 us  [attend_probs(): pl.pallas_call(probs_body, grid=(BLOCKS,), out_shape=(jax.ShapeDtypeStruc...]
    all_to_all x2 -> x0, starting transfers between devices: 9.94 us -> none  [the longest x1 5.04 us: local(): current = lax.all_to_all(sums, 'section', 0, 0, tiled=True)]
    ppermute x0 -> x6, starting transfers between devices: none -> 9.72 us  [turn(): return lax.ppermute(array, 'section', pairs)]
  transfers between devices with their start and end apart: 6 -> 11, of which waited for: 2 -> 7; matrix products, arithmetic and copies ran while one was open for 1% -> 0% of each run, Pallas kernels for 65% -> 38%
where the time goes in v1:
time: 281 us; the launch traced here: 276 us
  waiting for transfers between devices  115 us (41%)
  Pallas kernels  108 us (38%)
  starting transfers between devices  37 us (13%)
  between operations  14.1 us (5%)
    all_to_all x4, waiting for transfers between devices, exchange(): return lax.all_to_all(parts, 'seq', 0, 0, tiled=True)  76.4 us
    ppermute x6, waiting for transfers between devices, turn(): return lax.ppermute(array, 'section', pairs)  37.5 us
    pallas_call x1, Pallas kernels, attend_grads(): pl.pallas_call(grads_body, grid=(BLOCKS,), out_shape=jax.ShapeDtypeStruct...  27.4 us
    all_to_all x4, starting transfers between devices, exchange(): return lax.all_to_all(parts, 'seq', 0, 0, tiled=True)  27.3 us
    pallas_call x1, Pallas kernels, attend_probs(): pl.pallas_call(probs_body, grid=(BLOCKS,), out_shape=(jax.ShapeDtypeStruc...  20.4 us
    pallas_call x1, Pallas kernels, attend_values(): pl.pallas_call(values_body, grid=(BLOCKS,), out_shape=jax.ShapeDtypeStruc...  19.1 us
    pallas_call x1, Pallas kernels, norm_term(): pl.pallas_call(term_body, grid=(steps,), out_shape=tuple((jax.ShapeDtypeS...  15.3 us
    pallas_call x2, Pallas kernels, pack(): pl.pallas_call(pack_body, grid=(BATCH, per_seq), out_shape=jax.ShapeDtype...  11.7 us
  transfers between devices with their start and end apart: 11, of which 7 were waited for; matrix products, arithmetic and copies ran while one was open for 0% of the time, Pallas kernels for 38%

profile of v1, /device:TPU:10, one launch (start us, length us, event | category | flops | bytes accessed | tf_op | source)
XLA Modules:
  0.0 275.8 jit_solution(1998516426458741716)
XLA Ops:
  7.9 5.8 %pack.3 = bf16[32,64,640]{2,1,0:T(8,128)(2,1)} custom-call(bf16[2,64,8192]{2,1,0:T(8,128)(2,1)} %bitcast.22, bf16[2,64,1024]{2,1,0:T(8,128)(2,1)} %bitcast.26), custom_call_target="tpu_custom_call" | custom-call | flops 3000000000 | tf_op jit(solution)/shard_map/pack/pallas_call | solution.py:54
  13.7 8.5 %all-to-all-start.1 = ((bf16[32,64,640]{2,1,0:T(8,128)(2,1)}), bf16[32,64,640]{2,1,0:T(8,128)(2,1)S(1)}, u32[]{:S(2)}, u32[]{:S(2)}) async-start(bf16[32,64,640]{2,1,0:T(8,128)(2,1)} %pack.3), calls=%async_computation.1 | async-start | bytes 5242880 | tf_op jit(solution)/shard_map/all_to_all | solution.py:416
  22.2 5.9 %pack.2 = bf16[32,64,640]{2,1,0:T(8,128)(2,1)} custom-call(bf16[2,64,8192]{2,1,0:T(8,128)(2,1)} %bitcast.23, bf16[2,64,1024]{2,1,0:T(8,128)(2,1)} %bitcast.27), custom_call_target="tpu_custom_call" | custom-call | flops 3000000000 | tf_op jit(solution)/shard_map/pack/pallas_call | solution.py:54
  28.1 35.5 %all-to-all-done.1 = bf16[32,64,640]{2,1,0:T(8,128)(2,1)S(1)} async-done(((bf16[32,64,640]{2,1,0:T(8,128)(2,1)}), bf16[32,64,640]{2,1,0:T(8,128)(2,1)S(1)}, u32[]{:S(2)}, u32[]{:S(2)}) %all-to-all-start.1) | async-done | bytes 2621472 | tf_op jit(solution)/shard_map/all_to_all | solution.py:416
  63.6 6.4 %all-to-all-start = ((bf16[32,64,640]{2,1,0:T(8,128)(2,1)}), bf16[32,64,640]{2,1,0:T(8,128)(2,1)}, u32[]{:S(2)}, u32[]{:S(2)}) async-start(bf16[32,64,640]{2,1,0:T(8,128)(2,1)} %pack.2), calls=%async_computation | async-start | bytes 5242880 | tf_op jit(solution)/shard_map/all_to_all | solution.py:416
  70.1 20.4 %probs.1 = (bf16[8,4,256,512]{3,2,1,0:T(8,128)(2,1)}, bf16[8,8,256,512]{3,2,1,0:T(8,128)(2,1)}, f32[16,1,512]{2,1,0:T(1,128)}) custom-call(bf16[2048,640]{1,0:T(8,128)(2,1)} %bitcast.16, bf16[2048,640]{1,0:T(8,128)(2,1)} %bitcast.17), custom_call_target="tpu_custom_call" | custom-call | flops 17999998976 | tf_op jit(solution)/shard_map/probs/pallas_call | solution.py:154
  90.5 40.9 %all-to-all-done = bf16[32,64,640]{2,1,0:T(8,128)(2,1)} async-done(((bf16[32,64,640]{2,1,0:T(8,128)(2,1)}), bf16[32,64,640]{2,1,0:T(8,128)(2,1)}, u32[]{:S(2)}, u32[]{:S(2)}) %all-to-all-start) | async-done | bytes 2621472 | tf_op jit(solution)/shard_map/all_to_all | solution.py:416
  131.4 19.1 %values.1 = bf16[2048,128]{1,0:T(8,128)(2,1)} custom-call(bf16[2048,640]{1,0:T(8,128)(2,1)} %bitcast.3.g_ref.v_ref, bf16[8,4,256,512]{3,2,1,0:T(8,128)(2,1)} %get-tuple-element.16.low_ref, bf16[8,8,256,512]{3,2,1,0:T(8,128)(2,1)} %get-tuple-element.17.high_ref, f32[16,1,512]{2,1,0:T(1,128)} %get-tuple-element.18.l_ref), custom_call_target="tpu_custom_call" | custom-call | flops 10000000000 | tf_op jit(solution)/shard_map/values/pallas_call | solution.py:201
  150.6 4.9 %all-to-all-start.2 = ((bf16[32,64,128]{2,1,0:T(8,128)(2,1)}), bf16[32,64,128]{2,1,0:T(8,128)(2,1)S(1)}, u32[]{:S(2)}, u32[]{:S(2)}) async-start(bf16[32,64,128]{2,1,0:T(8,128)(2,1)} %bitcast.20), calls=%async_computation.2 | async-start | bytes 1048576 | tf_op jit(solution)/shard_map/all_to_all | solution.py:416
  155.4 27.4 %grads.1 = bf16[2048,640]{1,0:T(8,128)(2,1)} custom-call(bf16[2048,640]{1,0:T(8,128)(2,1)} %bitcast.18, bf16[2048,640]{1,0:T(8,128)(2,1)} %bitcast.3.g_ref.v_ref, bf16[2048,640]{1,0:T(8,128)(2,1)} %bitcast.19, bf16[2048,640]{1,0:T(8,128)(2,1)} %bitcast.3.g_ref.v_ref, bf16[8,4,256,512]{3,2,1,0:T(8,128)(2,1)} %get-tuple-element.16.low_ref, ...), custom_call_target="tpu_custom_call" | custom-call | flops 27000000512 | tf_op jit(solution)/shard_map/grads/pallas_call | solution.py:266
  183.6 7.5 %all-to-all-start.3 = ((bf16[32,64,640]{2,1,0:T(8,128)(2,1)}), bf16[32,64,640]{2,1,0:T(8,128)(2,1)S(1)}, u32[]{:S(2)}, u32[]{:S(2)}) async-start(bf16[32,64,640]{2,1,0:T(8,128)(2,1)} %bitcast.15), calls=%async_computation.3 | async-start | bytes 5242880 | tf_op jit(solution)/shard_map/all_to_all | solution.py:416
  191.2 15.3 %term.1 = (bf16[32,8192]{1,0:T(8,128)(2,1)}, bf16[32,8192]{1,0:T(8,128)(2,1)}, bf16[32,8192]{1,0:T(8,128)(2,1)}, bf16[32,8192]{1,0:T(8,128)(2,1)}) custom-call(s32[1]{0:T(128)} %bitcast.here_ref, bf16[32,64,128]{2,1,0:T(8,128)(2,1)} %copy-done.2, bf16[8192,1024]{1,0:T(8,128)(2,1)} %bitcast.21, bf16[128,8192]{1,0:T(8,128)(2,1)} %bitcast.24, ...), custom_call_target="tpu_custom_call" | custom-call | flops 12000000000 | tf_op jit(solution)/shard_map/term/pallas_call | solution.py:339
  206.4 1.8 collective-permute-start
  209.1 2.6 collective-permute-start.2
  211.7 19.6 %collective-permute-done.refs_1_ = bf16[32,8192]{1,0:T(8,128)(2,1)S(1)} collective-permute-done((bf16[32,8192]{1,0:T(8,128)(2,1)}, bf16[32,8192]{1,0:T(8,128)(2,1)S(1)}, u32[]{:S(2)}, u32[]{:S(2)}) %collective-permute-start) | collective-permute-done | bytes 524320 | tf_op jit(solution)/shard_map/ppermute | solution.py:421
  231.3 3.1 %collective-permute-done.2.refs_3_ = bf16[32,8192]{1,0:T(8,128)(2,1)} collective-permute-done((bf16[32,8192]{1,0:T(8,128)(2,1)}, bf16[32,8192]{1,0:T(8,128)(2,1)}, u32[]{:S(2)}, u32[]{:S(2)}) %collective-permute-start.2) | collective-permute-done | bytes 524320 | tf_op jit(solution)/shard_map/ppermute | solution.py:421
  234.4 4.1 %suffix_sums.1 = (bf16[32,8192]{1,0:T(8,128)(2,1)}, bf16[32,8192]{1,0:T(8,128)(2,1)}, bf16[32,8192]{1,0:T(8,128)(2,1)}, bf16[32,8192]{1,0:T(8,128)(2,1)}) custom-call(s32[1]{0:T(128)} %bitcast.here_ref, bf16[32,8192]{1,0:T(8,128)(2,1)} %get-tuple-element.19.refs_0_, bf16[32,8192]{1,0:T(8,128)(2,1)} %copy-done.4, bf16[32,8192]{1,0:T(8,128)(2,1)} %copy-done.5, ...), custom_call_target="tpu_custom_call" | custom-call | flops 2000000000 | tf_op jit(solution)/shard_map/suffix_sums/pallas_call | solution.py:380
  238.5 1.5 collective-permute-start.3
  241.1 1.7 collective-permute-start.5
  242.9 1.5 copy-done
  244.4 5.8 %unpack.1 = (bf16[2,64,8192]{2,1,0:T(8,128)(2,1)}, bf16[2,64,1024]{2,1,0:T(8,128)(2,1)}) custom-call(bf16[32,64,640]{2,1,0:T(8,128)(2,1)} %copy-done), custom_call_target="tpu_custom_call" | custom-call | flops 5000000000 | tf_op jit(solution)/shard_map/unpack/pallas_call | solution.py:79
  250.2 2.7 collective-permute-done.3.refs_1_
  252.9 11.0 %collective-permute-done.4.refs_2_ = bf16[32,8192]{1,0:T(8,128)(2,1)} collective-permute-done((bf16[32,8192]{1,0:T(8,128)(2,1)}, bf16[32,8192]{1,0:T(8,128)(2,1)}, u32[]{:S(2)}, u32[]{:S(2)}) %collective-permute-start.4) | collective-permute-done | bytes 524320 | tf_op jit(solution)/shard_map/ppermute | solution.py:421
  265.1 3.8 %place.1 = bf16[128,8192]{1,0:T(8,128)(2,1)} custom-call(s32[1]{0:T(128)} %bitcast.here_ref, bf16[32,8192]{1,0:T(8,128)(2,1)} %get-tuple-element.23.refs_0_, bf16[32,8192]{1,0:T(8,128)(2,1)} %copy-done.3, bf16[32,8192]{1,0:T(8,128)(2,1)} %collective-permute-done.4.refs_2_, bf16[32,8192]{1,0:T(8,128)(2,1)} %collective-permute-done.5.refs_3_), custom_call_target="tpu_custom_call" | custom-call | flops 2000000000 | tf_op jit(solution)/shard_map/place/pallas_call | solution.py:403
  (20 shorter events, 4.8 us)
Async XLA Ops:
  7.2 184.0 %all-gather.3.cloned.1.call-start = ((), (), s32[]{:S(2)}) async-start(), calls=%async_computation.4 | async-start | bytes 17301504 | tf_op jit(solution)/shard_map/all_gather | solution.py:427
  13.7 49.9 %all-to-all-start.1 = ((bf16[32,64,640]{2,1,0:T(8,128)(2,1)}), bf16[32,64,640]{2,1,0:T(8,128)(2,1)S(1)}, u32[]{:S(2)}, u32[]{:S(2)}) async-start(bf16[32,64,640]{2,1,0:T(8,128)(2,1)} %pack.3), calls=%async_computation.1 | async-start | bytes 5242880 | tf_op jit(solution)/shard_map/all_to_all | solution.py:416
  63.6 6.4 %copy-start.1 = (bf16[32,64,640]{2,1,0:T(8,128)(2,1)}, bf16[32,64,640]{2,1,0:T(8,128)(2,1)S(1)}, u32[]{:S(2)}) copy-start(bf16[32,64,640]{2,1,0:T(8,128)(2,1)S(1)} %all-to-all-done.1) | copy-start | bytes 7864324
  63.6 67.8 %all-to-all-start = ((bf16[32,64,640]{2,1,0:T(8,128)(2,1)}), bf16[32,64,640]{2,1,0:T(8,128)(2,1)}, u32[]{:S(2)}, u32[]{:S(2)}) async-start(bf16[32,64,640]{2,1,0:T(8,128)(2,1)} %pack.2), calls=%async_computation | async-start | bytes 5242880 | tf_op jit(solution)/shard_map/all_to_all | solution.py:416
  150.6 32.3 %all-to-all-start.2 = ((bf16[32,64,128]{2,1,0:T(8,128)(2,1)}), bf16[32,64,128]{2,1,0:T(8,128)(2,1)S(1)}, u32[]{:S(2)}, u32[]{:S(2)}) async-start(bf16[32,64,128]{2,1,0:T(8,128)(2,1)} %bitcast.20), calls=%async_computation.2 | async-start | bytes 1048576 | tf_op jit(solution)/shard_map/all_to_all | solution.py:416
  182.8 0.8 copy-start.2
  183.6 59.3 %all-to-all-start.3 = ((bf16[32,64,640]{2,1,0:T(8,128)(2,1)}), bf16[32,64,640]{2,1,0:T(8,128)(2,1)S(1)}, u32[]{:S(2)}, u32[]{:S(2)}) async-start(bf16[32,64,640]{2,1,0:T(8,128)(2,1)} %bitcast.15), calls=%async_computation.3 | async-start | bytes 5242880 | tf_op jit(solution)/shard_map/all_to_all | solution.py:416
  206.4 24.9 %collective-permute-start = (bf16[32,8192]{1,0:T(8,128)(2,1)}, bf16[32,8192]{1,0:T(8,128)(2,1)S(1)}, u32[]{:S(2)}, u32[]{:S(2)}) collective-permute-start(bf16[32,8192]{1,0:T(8,128)(2,1)} %get-tuple-element.20), channel_id=1, source_target_pairs={{0,32},{32,64},{64,96},{96,0},{1,33},{33,65},{65,97},{97,1},{2,34}... | collective-permute-start | bytes 1572872 | tf_op jit(solution)/shard_map/ppermute | solution.py:421
  208.2 23.1 %collective-permute-start.1 = (bf16[32,8192]{1,0:T(8,128)(2,1)}, bf16[32,8192]{1,0:T(8,128)(2,1)S(1)}, u32[]{:S(2)}, u32[]{:S(2)}) collective-permute-start(bf16[32,8192]{1,0:T(8,128)(2,1)} %get-tuple-element.21), channel_id=1, source_target_pairs={{0,64},{32,96},{64,0},{96,32},{1,65},{33,97},{65,1},{97,33},{2,66}... | collective-permute-start | bytes 1572872 | tf_op jit(solution)/shard_map/ppermute | solution.py:421
  209.1 25.2 %collective-permute-start.2 = (bf16[32,8192]{1,0:T(8,128)(2,1)}, bf16[32,8192]{1,0:T(8,128)(2,1)}, u32[]{:S(2)}, u32[]{:S(2)}) collective-permute-start(bf16[32,8192]{1,0:T(8,128)(2,1)} %get-tuple-element.22), channel_id=1, source_target_pairs={{0,96},{32,0},{64,32},{96,64},{1,97},{33,1},{65,33},{97,65},{2,98}... | collective-permute-start | bytes 1572872 | tf_op jit(solution)/shard_map/ppermute | solution.py:421
  231.3 3.1 %copy-start.4 = (bf16[32,8192]{1,0:T(8,128)(2,1)}, bf16[32,8192]{1,0:T(8,128)(2,1)S(1)}, u32[]{:S(2)}) copy-start(bf16[32,8192]{1,0:T(8,128)(2,1)S(1)} %collective-permute-done.refs_1_) | copy-start | bytes 1572868
  231.3 3.1 %copy-start.5 = (bf16[32,8192]{1,0:T(8,128)(2,1)}, bf16[32,8192]{1,0:T(8,128)(2,1)S(1)}, u32[]{:S(2)}) copy-start(bf16[32,8192]{1,0:T(8,128)(2,1)S(1)} %collective-permute-done.1.refs_2_) | copy-start | bytes 1572868
  238.5 14.4 %collective-permute-start.3 = (bf16[32,8192]{1,0:T(8,128)(2,1)}, bf16[32,8192]{1,0:T(8,128)(2,1)S(1)}, u32[]{:S(2)}, u32[]{:S(2)}) collective-permute-start(bf16[32,8192]{1,0:T(8,128)(2,1)} %get-tuple-element.24), channel_id=1, source_target_pairs={{0,96},{32,0},{64,32},{96,64},{1,97},{33,1},{65,33},{97,65},{2,98}... | collective-permute-start | bytes 1572872 | tf_op jit(solution)/shard_map/ppermute | solution.py:421
  240.0 23.9 %collective-permute-start.4 = (bf16[32,8192]{1,0:T(8,128)(2,1)}, bf16[32,8192]{1,0:T(8,128)(2,1)}, u32[]{:S(2)}, u32[]{:S(2)}) collective-permute-start(bf16[32,8192]{1,0:T(8,128)(2,1)} %get-tuple-element.25), channel_id=1, source_target_pairs={{0,64},{32,96},{64,0},{96,32},{1,65},{33,97},{65,1},{97,33},{2,66}... | collective-permute-start | bytes 1572872 | tf_op jit(solution)/shard_map/ppermute | solution.py:421
  241.1 23.9 %collective-permute-start.5 = (bf16[32,8192]{1,0:T(8,128)(2,1)}, bf16[32,8192]{1,0:T(8,128)(2,1)}, u32[]{:S(2)}, u32[]{:S(2)}) collective-permute-start(bf16[32,8192]{1,0:T(8,128)(2,1)} %get-tuple-element.26), channel_id=1, source_target_pairs={{0,32},{32,64},{64,96},{96,0},{1,33},{33,65},{65,97},{97,1},{2,34}... | collective-permute-start | bytes 1572872 | tf_op jit(solution)/shard_map/ppermute | solution.py:421
  242.9 1.5 copy-start
  252.9 12.2 %copy-start.3 = (bf16[32,8192]{1,0:T(8,128)(2,1)}, bf16[32,8192]{1,0:T(8,128)(2,1)S(1)}, u32[]{:S(2)}) copy-start(bf16[32,8192]{1,0:T(8,128)(2,1)S(1)} %collective-permute-done.3.refs_1_) | copy-start | bytes 1572868
Sparse Core Ops, SparseCore 0:
  10.3 127.6 all-gather.2
